TPU v7x, 128 devices: a whole 4x4x4 slice. The times are simulated.
128 devices in a mesh: row: 32 (over z, y, core), col: 4 (over x).
Axes of the slice: x: 4, y: 4, z: 4, core: 2. Of those that a mesh axis runs over, the one named last changes fastest.
Arguments:
- tokens: bfloat16 [16384, 2048], P('row', 'col'), may hold values from -6 to 6
- cotangent: bfloat16 [16384, 2048], P('row', 'col'), may hold values from -6 to 6
- destination: int32 [16384], P('row'), may hold values from 0 to 16383, as said below
- segment_ids: int32 [16384], P('row'), may hold values from 0 to 7, as said below
- attn_gain: float32 [2048], replicated, may hold values from 0.5 to 1.5
- w_query: bfloat16 [2048, 2048], P('row', 'col'), may hold values from -0.125 to 0.125
- w_key: bfloat16 [2048, 256], P('row', 'col'), may hold values from -0.125 to 0.125
- w_value: bfloat16 [2048, 256], P('row', 'col'), may hold values from -0.125 to 0.125
- w_output: bfloat16 [2048, 2048], P('row', 'col'), may hold values from -0.5 to 0.5
- ffn_gain: float32 [2048], replicated, may hold values from 0.5 to 1.5
- w_gate: bfloat16 [2048, 5632], P('row', 'col'), may hold values from -0.125 to 0.125
- w_up: bfloat16 [2048, 5632], P('row', 'col'), may hold values from -0.125 to 0.125
- w_down: bfloat16 [2048, 5632], P('row', 'col'), may hold values from -0.078125 to 0.078125
Outputs:
- output: bfloat16 [16384, 2048], P('row', 'col')
- input_grad: bfloat16 [16384, 2048], P('row', 'col')
- attn_gain_grad: float32 [2048], P('row')
- w_query_grad: float32 [2048, 2048], P('row', 'col')
- w_key_grad: float32 [2048, 256], P('row', 'col')
- w_value_grad: float32 [2048, 256], P('row', 'col')
- w_output_grad: float32 [2048, 2048], P('row', 'col')
- ffn_gain_grad: float32 [2048], P('row')
- w_gate_grad: float32 [2048, 5632], P('row', 'col')
- w_up_grad: float32 [2048, 5632], P('row', 'col')
- w_down_grad: float32 [2048, 5632], P('row', 'col')
Inputs may be any that keep to these rules, and one draw needn't show every extreme that they name: `destination`: A permutation; the tokens of each aligned block of 512 arriving tokens go to exactly 16 places in each aligned block of 512 balanced places. `segment_ids`: within each aligned block of 512 places the ids start at 0 and rise by one where a new sequence begins, so a block holds at most 8 sequences; in every draw some block holds a single sequence of 512 tokens and some block holds 8 sequences.
All inputs are finite; a program needn't handle non-finite values.
Results may differ from a plain program's by a relative error of at most 0.028.
Values may be sent and summed in bfloat16 or wider, within the bound.
No kernel may reach another device: no remote copies, remote signals or barrier semaphores. Data moves between devices by JAX's collectives and lax.ppermute only.
A program may use at most 128 MiB of HBM per device.

v0:
```python
from functools import partial
import jax
import jax.numpy as jnp
from jax import lax
from jax.sharding import PartitionSpec as P

HEADS = 32
KV = 4
HD = 64
EPS = 1e-05
ROPE_BASE = 10000.0


def rope_tables(positions):
    half_width = HD // 2
    freqs = ROPE_BASE ** (-(jnp.arange(half_width, dtype=jnp.float32) * 2.0 / HD))
    angles = positions.astype(jnp.float32)[:, None] * freqs[None, :]
    return (jnp.cos(angles)[:, None, :], jnp.sin(angles)[:, None, :])


def rotate(values, cosine, sine):
    half_width = values.shape[-1] // 2
    first = values[..., :half_width]
    second = values[..., half_width:]
    return jnp.concatenate(
        [first * cosine - second * sine, second * cosine + first * sine], axis=-1
    )


def rotate_back(grads, cosine, sine):
    half_width = grads.shape[-1] // 2
    first = grads[..., :half_width]
    second = grads[..., half_width:]
    return jnp.concatenate(
        [first * cosine + second * sine, second * cosine - first * sine], axis=-1
    )


def positions_of(segment_ids):
    index = jnp.arange(segment_ids.shape[0], dtype=jnp.int32)
    change = jnp.concatenate([jnp.ones((1,), dtype=jnp.bool_), segment_ids[1:] != segment_ids[:-1]])
    starts = jnp.where(change, index, jnp.zeros_like(index))
    return index - lax.cummax(starts, axis=0)


def allowed_pairs(segment_ids):
    index = jnp.arange(segment_ids.shape[0], dtype=jnp.int32)
    return (segment_ids[:, None] == segment_ids[None, :]) & (index[None, :] <= index[:, None])


def rms_scale(values):
    return lax.rsqrt(jnp.mean(values * values, axis=-1, keepdims=True) + EPS)


def norm_back(values, inv_root, gain, grads):
    normed = values * inv_root
    scaled = grads * gain
    result = inv_root * (scaled - normed * jnp.mean(scaled * normed, axis=-1, keepdims=True))
    return (result, jnp.sum(grads * normed, axis=0))


def matmul(left, right):
    return jnp.dot(left, right, preferred_element_type=jnp.float32)


def head_scores(query_head, key_head, allowed, scale_factor):
    scores = matmul(query_head, key_head.T) * scale_factor
    return jnp.where(allowed, scores, -1e30)


def head_forward(inputs, key_heads, value_heads, allowed, scale_factor):
    query_head, kv_slot = inputs
    scores = head_scores(query_head, key_heads[kv_slot], allowed, scale_factor)
    peak = jnp.max(scores, axis=-1, keepdims=True)
    expo = jnp.exp(scores - peak)
    total = jnp.sum(expo, axis=-1, keepdims=True)
    probs = expo / total
    mixed = matmul(probs.astype(jnp.bfloat16), value_heads[kv_slot])
    return (mixed, (peak + jnp.log(total))[:, 0])


def head_backward(inputs, key_heads, value_heads, allowed, scale_factor):
    query_head, kv_slot, grad_head, log_total = inputs
    key_head = key_heads[kv_slot]
    value_head = value_heads[kv_slot]
    scores = head_scores(query_head, key_head, allowed, scale_factor)
    probs = jnp.exp(scores - log_total[:, None])
    prob_grad = matmul(grad_head, value_head.T)
    value_grad = matmul(probs.astype(jnp.bfloat16).T, grad_head)
    inner = jnp.sum(probs * prob_grad, axis=-1, keepdims=True)
    score_grad = (probs * (prob_grad - inner)).astype(jnp.bfloat16)
    query_grad = matmul(score_grad, key_head) * scale_factor
    key_grad = matmul(score_grad.T, query_head) * scale_factor
    return (query_grad, key_grad, value_grad)


def body(
    tokens,
    cotangent,
    destination,
    segment_ids,
    attn_gain,
    w_query,
    w_key,
    w_value,
    w_output,
    ffn_gain,
    w_gate,
    w_up,
    w_down,
):
    row_count = tokens.shape[0]
    quarter = tokens.shape[1]
    col_start = lax.axis_index("col") * quarter
    group_size = HEADS // KV
    send_order = jnp.argsort(destination)
    slot_ids = destination[send_order] % row_count
    arrived_rows, arrived_grads, arrived_slots = (
        lax.all_to_all(tokens[send_order], "row", split_axis=0, concat_axis=0, tiled=True),
        lax.all_to_all(cotangent[send_order], "row", split_axis=0, concat_axis=0, tiled=True),
        lax.all_to_all(slot_ids, "row", split_axis=0, concat_axis=0, tiled=True),
    )
    placing = jnp.argsort(arrived_slots)
    full_rows, full_grads = (
        lax.all_gather(arrived_rows[placing], "col", axis=1, tiled=True),
        lax.all_gather(arrived_grads[placing], "col", axis=1, tiled=True),
    )
    query_w, key_w, value_w, output_w = (
        lax.all_gather(w_query, "row", axis=0, tiled=True),
        lax.all_gather(w_key, "row", axis=0, tiled=True),
        lax.all_gather(w_value, "row", axis=0, tiled=True),
        lax.all_gather(w_output, "row", axis=0, tiled=True),
    )
    cosine, sine = rope_tables(positions_of(segment_ids))
    allowed = allowed_pairs(segment_ids)
    rows_wide = full_rows.astype(jnp.float32)
    inv_one = rms_scale(rows_wide)
    normed_one = (rows_wide * inv_one * attn_gain).astype(jnp.bfloat16)
    query = matmul(normed_one, query_w)
    key_raw = matmul(normed_one, key_w)
    value_raw = matmul(normed_one, value_w)
    query_heads_count = query.shape[1] // HD
    kv_count = key_raw.shape[1] // HD
    query_rot = (
        rotate(query.reshape(row_count, query_heads_count, HD), cosine, sine)
        .astype(jnp.bfloat16)
        .transpose(1, 0, 2)
    )
    key_rot = (
        rotate(key_raw.reshape(row_count, kv_count, HD), cosine, sine)
        .astype(jnp.bfloat16)
        .transpose(1, 0, 2)
    )
    value_heads = value_raw.astype(jnp.bfloat16).reshape(row_count, kv_count, HD).transpose(1, 0, 2)
    kv_slots = jnp.arange(query_heads_count, dtype=jnp.int32) // group_size
    scale_factor = HD ** (-0.5)
    mixed_heads, log_totals = lax.map(
        partial(
            head_forward,
            key_heads=key_rot,
            value_heads=value_heads,
            allowed=allowed,
            scale_factor=scale_factor,
        ),
        (query_rot, kv_slots),
    )
    mixed = (
        mixed_heads.transpose(1, 0, 2)
        .reshape(row_count, query_heads_count * HD)
        .astype(jnp.bfloat16)
    )
    attn_terms = matmul(mixed, output_w.T)
    attn_full = lax.psum(attn_terms, "col")
    resid = rows_wide + attn_full
    inv_two = rms_scale(resid)
    normed_two = (resid * inv_two * ffn_gain).astype(jnp.bfloat16)
    resid_part = lax.dynamic_slice_in_dim(resid, col_start, quarter, 1)
    gate_w, up_w, down_w = (
        lax.all_gather(w_gate, "row", axis=0, tiled=True),
        lax.all_gather(w_up, "row", axis=0, tiled=True),
        lax.all_gather(w_down, "row", axis=0, tiled=True),
    )
    gate = matmul(normed_two, gate_w)
    upper = matmul(normed_two, up_w)
    sigmoid_gate = jax.nn.sigmoid(gate)
    activ = (gate * sigmoid_gate * upper).astype(jnp.bfloat16)
    ffn_share = lax.psum_scatter(
        matmul(activ, down_w.T).astype(jnp.bfloat16), "col", scatter_dimension=1, tiled=True
    ).astype(jnp.float32)
    output_share = (resid_part + ffn_share).astype(jnp.bfloat16)
    gate_w, up_w, down_w = (
        lax.all_gather(w_gate, "row", axis=0, tiled=True),
        lax.all_gather(w_up, "row", axis=0, tiled=True),
        lax.all_gather(w_down, "row", axis=0, tiled=True),
    )
    down_weight_grad = matmul(full_grads.T, activ)
    act_grad = matmul(full_grads, down_w)
    gate_grad = (act_grad * upper * sigmoid_gate * (1.0 + gate * (1.0 - sigmoid_gate))).astype(
        jnp.bfloat16
    )
    up_grad = (act_grad * gate * sigmoid_gate).astype(jnp.bfloat16)
    gate_weight_grad = matmul(normed_two.T, gate_grad)
    up_weight_grad = matmul(normed_two.T, up_grad)
    normed_terms_two = matmul(gate_grad, gate_w.T) + matmul(up_grad, up_w.T)
    normed_grad_two = lax.psum(normed_terms_two, "col")
    resid_norm_grad, ffn_gain_grad = norm_back(resid, inv_two, ffn_gain, normed_grad_two)
    resid_grad = full_grads.astype(jnp.float32) + resid_norm_grad
    attn_grad_low = resid_grad.astype(jnp.bfloat16)
    ffn_results = (
        lax.psum_scatter(
            gate_weight_grad.astype(jnp.bfloat16), "row", scatter_dimension=0, tiled=True
        ).astype(jnp.float32),
        lax.psum_scatter(
            up_weight_grad.astype(jnp.bfloat16), "row", scatter_dimension=0, tiled=True
        ).astype(jnp.float32),
        lax.psum_scatter(
            down_weight_grad.astype(jnp.bfloat16), "row", scatter_dimension=0, tiled=True
        ).astype(jnp.float32),
        lax.psum_scatter(
            ffn_gain_grad.astype(jnp.bfloat16), "row", scatter_dimension=0, tiled=True
        ).astype(jnp.float32),
    )
    query_w, key_w, value_w, output_w = (
        lax.all_gather(w_query, "row", axis=0, tiled=True),
        lax.all_gather(w_key, "row", axis=0, tiled=True),
        lax.all_gather(w_value, "row", axis=0, tiled=True),
        lax.all_gather(w_output, "row", axis=0, tiled=True),
    )
    output_weight_grad = matmul(attn_grad_low.T, mixed)
    mixed_grad = matmul(attn_grad_low, output_w).astype(jnp.bfloat16)
    mixed_grad_heads = mixed_grad.reshape(row_count, query_heads_count, HD).transpose(1, 0, 2)
    query_grads, key_grads, value_grads = lax.map(
        partial(
            head_backward,
            key_heads=key_rot,
            value_heads=value_heads,
            allowed=allowed,
            scale_factor=scale_factor,
        ),
        (query_rot, kv_slots, mixed_grad_heads, log_totals),
    )
    query_grad = (
        rotate_back(query_grads.transpose(1, 0, 2), cosine, sine)
        .reshape(row_count, query_heads_count * HD)
        .astype(jnp.bfloat16)
    )
    key_sum = key_grads.reshape(kv_count, group_size, row_count, HD).sum(axis=1).transpose(1, 0, 2)
    key_grad = (
        rotate_back(key_sum, cosine, sine).reshape(row_count, kv_count * HD).astype(jnp.bfloat16)
    )
    value_sum = (
        value_grads.reshape(kv_count, group_size, row_count, HD).sum(axis=1).transpose(1, 0, 2)
    )
    value_grad = value_sum.reshape(row_count, kv_count * HD).astype(jnp.bfloat16)
    query_weight_grad = matmul(normed_one.T, query_grad)
    key_weight_grad = matmul(normed_one.T, key_grad)
    value_weight_grad = matmul(normed_one.T, value_grad)
    normed_terms_one = (
        matmul(query_grad, query_w.T) + matmul(key_grad, key_w.T) + matmul(value_grad, value_w.T)
    )
    normed_grad_one = lax.psum(normed_terms_one.astype(jnp.bfloat16), "col").astype(jnp.float32)
    rows_norm_grad, attn_gain_grad = norm_back(rows_wide, inv_one, attn_gain, normed_grad_one)
    rows_grad = resid_grad + rows_norm_grad
    input_share = lax.dynamic_slice_in_dim(rows_grad, col_start, quarter, 1).astype(jnp.bfloat16)
    attn_results = (
        lax.psum_scatter(
            query_weight_grad.astype(jnp.bfloat16), "row", scatter_dimension=0, tiled=True
        ).astype(jnp.float32),
        lax.psum_scatter(
            key_weight_grad.astype(jnp.bfloat16), "row", scatter_dimension=0, tiled=True
        ).astype(jnp.float32),
        lax.psum_scatter(
            value_weight_grad.astype(jnp.bfloat16), "row", scatter_dimension=0, tiled=True
        ).astype(jnp.float32),
        lax.psum_scatter(
            output_weight_grad.astype(jnp.bfloat16), "row", scatter_dimension=0, tiled=True
        ).astype(jnp.float32),
        lax.psum_scatter(
            attn_gain_grad.astype(jnp.bfloat16), "row", scatter_dimension=0, tiled=True
        ).astype(jnp.float32),
    )
    back_rows, back_grads = (
        lax.all_to_all(output_share[arrived_slots], "row", split_axis=0, concat_axis=0, tiled=True),
        lax.all_to_all(input_share[arrived_slots], "row", split_axis=0, concat_axis=0, tiled=True),
    )
    restore = jnp.argsort(send_order)
    return (
        back_rows[restore],
        back_grads[restore],
        attn_results[4],
        attn_results[0],
        attn_results[1],
        attn_results[2],
        attn_results[3],
        ffn_results[3],
        ffn_results[0],
        ffn_results[1],
        ffn_results[2],
    )


def solution(mesh):
    placed = (
        P("row", "col"),
        P("row", "col"),
        P("row"),
        P("row"),
        P(),
        P("row", "col"),
        P("row", "col"),
        P("row", "col"),
        P("row", "col"),
        P(),
        P("row", "col"),
        P("row", "col"),
        P("row", "col"),
    )
    return jax.shard_map(
        body,
        mesh=mesh,
        in_specs=placed,
        out_specs=(
            P("row", "col"),
            P("row", "col"),
            P("row"),
            P("row", "col"),
            P("row", "col"),
            P("row", "col"),
            P("row", "col"),
            P("row"),
            P("row", "col"),
            P("row", "col"),
            P("row", "col"),
        ),
        check_vma=False,
    )
```

profile of v0, /device:TPU:0, one launch (start us, length us, event | category | flops | bytes accessed | tf_op | source)
XLA Modules:
  0.0 1312.7 jit_solution(15525933860058886407)
XLA Ops:
  16.6 8.4 all-to-all-start.1
  53.0 22.4 %all_gather.36 = bf16[2048,64]{1,0:T(8,128)(2,1)S(1)} all-gather(bf16[64,64]{1,0:T(8,128)(2,1)S(1)} %copy-done.22), channel_id=1, replica_groups=mesh['row'=32,'col'=4] {'row'}, dimensions={0}, use_global_device_ids=true | all-gather | bytes 270336 | tf_op jit(solution)/shard_map/all_gather | solution.py:130
  75.5 26.7 %all_gather.37 = bf16[2048,64]{1,0:T(8,128)(2,1)} all-gather(bf16[64,64]{1,0:T(8,128)(2,1)S(1)} %copy-done.23), channel_id=1, replica_groups=mesh['row'=32,'col'=4] {'row'}, dimensions={0}, use_global_device_ids=true | all-gather | bytes 270336 | tf_op jit(solution)/shard_map/all_gather | solution.py:131
  111.2 14.4 %all-gather.10.cloned.1.call-done = bf16[2048,512]{1,0:T(8,128)(2,1)} async-done(((bf16[64,512]{1,0:T(8,128)(2,1)}), bf16[2048,512]{1,0:T(8,128)(2,1)}) %all-gather.10.cloned.1.call-update) | async-done | bytes 2097168 | tf_op jit(solution)/shard_map/all_gather | solution.py:129
  129.4 24.0 %while.32 = (s32[]{:T(128)}, bf16[8,512,64]{1,2,0:T(8,128)(2,1)S(1)}, f32[8,512]{1,0:T(8,128)}, bf16[8,512,64]{2,1,0:T(8,128)(2,1)S(1)}, bf16[1,512,64]{2,1,0:T(...) while((s32[]{:T(128)}, bf16[8,512,64]{1,2,0:T(8,128)(2,1)S(1)}, ...), condition=%wide.region_8.9_spmd.clone.clone, body=%wide.region_5.8_spmd.clone.sunk.clone | while | flops 69991936 | bytes 3695189 | solution.py:157
  153.4 17.8 %all-gather.12.cloned.1.call-done = bf16[2048,512]{1,0:T(8,128)(2,1)} async-done(((bf16[64,512]{1,0:T(8,128)(2,1)}), bf16[2048,512]{1,0:T(8,128)(2,1)}) %all-gather.12.cloned.1.call-update) | async-done | bytes 2097168 | tf_op jit(solution)/shard_map/all_gather | solution.py:132
  180.0 17.1 %all_to_all.60 = bf16[32,16,512]{2,1,0:T(8,128)(2,1)S(1)} all-to-all(bf16[32,16,512]{2,1,0:T(8,128)(2,1)} %bitcast.194), channel_id=1, replica_groups=mesh['row'=32,'col'=4] {'row'}, dimensions={0} | all-to-all | bytes 1048576 | tf_op jit(solution)/shard_map/all_to_all | solution.py:120
  201.1 67.2 %all-reduce.7.cloned.1.call-done = f32[512,2048]{1,0:T(8,128)} async-done(((f32[512,2048]{1,0:T(8,128)}), f32[512,2048]{1,0:T(8,128)}) %all-reduce.7.cloned.1.call-update) | async-done | bytes 4194320 | tf_op jit(solution)/shard_map/psum | solution.py:173
  274.8 44.2 %all-gather.14.cloned.1.call-done = bf16[2048,1408]{1,0:T(8,128)(2,1)} async-done(((bf16[64,1408]{1,0:T(8,128)(2,1)}), bf16[2048,1408]{1,0:T(8,128)(2,1)}) %all-gather.14.cloned.1.call-update) | async-done | bytes 5767184 | tf_op jit(solution)/shard_map/all_gather | solution.py:179
  319.0 8.3 fusion.76
  327.3 41.5 %all-gather.16.cloned.1.call-done = bf16[2048,1408]{1,0:T(8,128)(2,1)} async-done(((bf16[64,1408]{1,0:T(8,128)(2,1)}), bf16[2048,1408]{1,0:T(8,128)(2,1)}) %all-gather.16.cloned.1.call-update) | async-done | bytes 5767184 | tf_op jit(solution)/shard_map/all_gather | solution.py:180
  368.8 8.3 fusion.77
  377.1 23.9 %all-gather.22.cloned.1.call-done = bf16[512,2048]{1,0:T(8,128)(2,1)} async-done(((bf16[512,512]{1,0:T(8,128)(2,1)}), bf16[512,2048]{1,0:T(8,128)(2,1)}) %all-gather.22.cloned.1.call-update) | async-done | bytes 2097168 | tf_op jit(solution)/shard_map/all_gather | solution.py:126
  400.9 51.0 %all-gather.18.cloned.1.call-done = bf16[2048,1408]{1,0:T(8,128)(2,1)} async-done(((bf16[64,1408]{1,0:T(8,128)(2,1)}), bf16[2048,1408]{1,0:T(8,128)(2,1)}) %all-gather.18.cloned.1.call-update) | async-done | bytes 5767184 | tf_op jit(solution)/shard_map/all_gather | solution.py:181
  452.0 10.3 multiply_convert_fusion.3
  474.2 7.9 convolution_convert_fusion.5
  482.2 83.7 %all-reduce.9.cloned.1.call-done = f32[512,2048]{1,0:T(8,128)} async-done(((f32[512,2048]{1,0:T(8,128)}), f32[512,2048]{1,0:T(8,128)}) %all-reduce.9.cloned.1.call-update) | async-done | bytes 4194320 | tf_op jit(solution)/shard_map/psum | solution.py:205
  579.3 65.5 %while.33 = (s32[]{:T(128)}, f32[8,512,64]{1,2,0:T(8,128)}, f32[8,512,64]{1,2,0:T(8,128)}, f32[8,512,64]{1,2,0:T(8,128)}, bf16[8,512,64]{2,1,0:T(8,128)(2,1)}, /...) while((s32[]{:T(128)}, f32[8,512,64]{1,2,0:T(8,128)}, ...), condition=%wide.region_17.18_spmd.clone.clone, body=%wide.region_15.17_spmd.clone.sunk.clone | while | flops 170982912 | bytes 8996457 | solution.py:232
  667.5 8.0 convolution_convert_fusion.2
  675.5 8.1 convolution_convert_fusion.1
  683.9 7.9 convolution_convert_fusion
  696.3 7.3 all-to-all-start.2
  703.5 10.4 all-reduce.11.cloned.1.call-done
  721.0 7.3 all-to-all-start.4
  733.4 61.5 %reduce-scatter.13.cloned.1.call-done = bf16[64,64]{1,0:T(8,128)(2,1)} async-done(((bf16[2048,64]{1,0:T(8,128)(2,1)}), bf16[64,64]{1,0:T(8,128)(2,1)}) %reduce-scatter.13.cloned.1.call-update) | async-done | bytes 8208 | tf_op jit(solution)/shard_map/reduce_scatter | solution.py:269
  796.2 78.5 %reduce-scatter.15.cloned.1.call-done = bf16[64,64]{1,0:T(8,128)(2,1)} async-done(((bf16[2048,64]{1,0:T(8,128)(2,1)}), bf16[64,64]{1,0:T(8,128)(2,1)}) %reduce-scatter.15.cloned.1.call-update) | async-done | bytes 8208 | tf_op jit(solution)/shard_map/reduce_scatter | solution.py:272
  878.7 64.4 %all-reduce.2 = (bf16[2048]{0:T(1024)(128)(2,1)S(1)}, bf16[2048]{0:T(1024)(128)(2,1)S(1)}) all-reduce(bf16[2048]{0:T(1024)(128)(2,1)S(1)} %get-tuple-element.249, bf16[2048]{0:T(1024)(128)(2,1)S(1)} %copy-done.20), channel_id=5, replica_groups=mesh['row'=32,'col'=4] {'row'}, use_global_device_ids=true, to_apply=%region_23.24.clone | all-reduce | flops 4096 | bytes 16384
  946.4 10.0 reduce-scatter.11.cloned.1.call-done
  957.9 80.2 %reduce-scatter.17.cloned.1.call-done = bf16[64,512]{1,0:T(8,128)(2,1)} async-done(((bf16[2048,512]{1,0:T(8,128)(2,1)}), bf16[64,512]{1,0:T(8,128)(2,1)}) %reduce-scatter.17.cloned.1.call-update) | async-done | bytes 65552 | tf_op jit(solution)/shard_map/reduce_scatter | solution.py:275
  1039.6 86.9 %reduce-scatter.19.cloned.1.call-done = bf16[64,1408]{1,0:T(8,128)(2,1)} async-done(((bf16[2048,1408]{1,0:T(8,128)(2,1)}), bf16[64,1408]{1,0:T(8,128)(2,1)}) %reduce-scatter.19.cloned.1.call-update) | async-done | bytes 180240 | tf_op jit(solution)/shard_map/reduce_scatter | solution.py:210
  1128.2 87.2 %reduce-scatter.21.cloned.1.call-done = bf16[64,1408]{1,0:T(8,128)(2,1)} async-done(((bf16[2048,1408]{1,0:T(8,128)(2,1)}), bf16[64,1408]{1,0:T(8,128)(2,1)}) %reduce-scatter.21.cloned.1.call-update) | async-done | bytes 180240 | tf_op jit(solution)/shard_map/reduce_scatter | solution.py:213
  1217.0 86.7 %reduce-scatter.23.cloned.1.call-done = bf16[64,1408]{1,0:T(8,128)(2,1)} async-done(((bf16[2048,1408]{1,0:T(8,128)(2,1)}), bf16[64,1408]{1,0:T(8,128)(2,1)}) %reduce-scatter.23.cloned.1.call-update) | async-done | bytes 180240 | tf_op jit(solution)/shard_map/reduce_scatter | solution.py:216
  (298 shorter events, 239.0 us)
Async XLA Ops:
  16.6 15.7 %all-to-all-start.1 = ((s32[32,16,1]{1,2,0:T(1,128)}), s32[32,16,1]{1,2,0:T(1,128)S(1)}, u32[]{:S(2)}, u32[]{:S(2)}) async-start(s32[32,16,1]{1,2,0:T(1,128)} %bitcast.2), calls=%async_computation.1 | async-start | bytes 32768 | tf_op jit(solution)/shard_map/all_to_all | solution.py:121
  27.7 25.3 %copy-start.22 = (bf16[64,64]{1,0:T(8,128)(2,1)S(1)}, bf16[64,64]{1,0:T(8,128)(2,1)}, u32[]{:S(2)}) copy-start(bf16[64,64]{1,0:T(8,128)(2,1)} %param.23) | copy-start | bytes 24580
  27.7 47.8 %copy-start.23 = (bf16[64,64]{1,0:T(8,128)(2,1)S(1)}, bf16[64,64]{1,0:T(8,128)(2,1)}, u32[]{:S(2)}) copy-start(bf16[64,64]{1,0:T(8,128)(2,1)} %param.24) | copy-start | bytes 24580
  32.3 15.7 %all-to-all-start = ((bf16[32,16,512]{2,1,0:T(8,128)(2,1)}), bf16[32,16,512]{2,1,0:T(8,128)(2,1)S(1)}, u32[]{:S(2)}, u32[]{:S(2)}) async-start(bf16[32,16,512]{2,1,0:T(8,128)(2,1)} %bitcast), calls=%async_computation | async-start | bytes 1048576 | tf_op jit(solution)/shard_map/all_to_all | solution.py:119
  36.2 66.3 %all-gather.20.cloned.1.call-start = ((), (), s32[]{:S(2)}) async-start(), calls=%async_computation.29 | async-start | bytes 2621440 | tf_op jit(solution)/shard_map/all_gather | solution.py:125
  48.0 56.8 %copy-start.24 = (f32[2048]{0:T(1024)S(1)}, f32[2048]{0:T(1024)}, u32[]{:S(2)}) copy-start(f32[2048]{0:T(1024)} %param.21) | copy-start | bytes 24580
  50.6 75.0 %all-gather.10.cloned.1.call-start = ((), (), s32[]{:S(2)}) async-start(), calls=%async_computation.13 | async-start | bytes 2162688 | tf_op jit(solution)/shard_map/all_gather | solution.py:129
  51.4 119.8 %all-gather.12.cloned.1.call-start = ((), (), s32[]{:S(2)}) async-start(), calls=%async_computation.14 | async-start | bytes 2162688 | tf_op jit(solution)/shard_map/all_gather | solution.py:132
  52.1 216.2 %all-reduce.7.cloned.1.call-start = ((), (), s32[]{:S(2)}) async-start(), calls=%async_computation.15 | async-start | bytes 8388608 | tf_op jit(solution)/shard_map/psum | solution.py:173
  52.2 55.4 %copy-start.29 = (f32[32]{0:T(128)}, f32[32]{0:T(128)S(1)}, u32[]{:S(2)}) copy-start(f32[32]{0:T(128)S(1)} %negate_power_fusion) | copy-start | bytes 388
  53.0 54.5 %copy-start.15 = (f32[512]{0:T(512)}, f32[512]{0:T(512)S(1)}, u32[]{:S(2)}) copy-start(f32[512]{0:T(512)S(1)} %fusion.70) | copy-start | bytes 6148
  75.5 34.8 %copy-start.10 = (bf16[2048,64]{1,0:T(8,128)(2,1)}, bf16[2048,64]{1,0:T(8,128)(2,1)S(1)}, u32[]{:S(2)}) copy-start(bf16[2048,64]{1,0:T(8,128)(2,1)S(1)} %all_gather.36) | copy-start | bytes 786436
  176.1 142.8 %all-gather.14.cloned.1.call-start = ((), (), s32[]{:S(2)}) async-start(), calls=%async_computation.16 | async-start | bytes 5947392 | tf_op jit(solution)/shard_map/all_gather | solution.py:179
  176.7 192.1 %all-gather.16.cloned.1.call-start = ((), (), s32[]{:S(2)}) async-start(), calls=%async_computation.17 | async-start | bytes 5947392 | tf_op jit(solution)/shard_map/all_gather | solution.py:180
  177.3 223.6 %all-gather.22.cloned.1.call-start = ((), (), s32[]{:S(2)}) async-start(), calls=%async_computation.30 | async-start | bytes 2621440 | tf_op jit(solution)/shard_map/all_gather | solution.py:126
  180.0 88.3 %copy-start.7 = (bf16[512,2048]{1,0:T(8,128)(2,1)S(1)}, bf16[512,2048]{1,0:T(8,128)(2,1)}, u32[]{:S(2)}) copy-start(bf16[512,2048]{1,0:T(8,128)(2,1)} %all-gather.20.cloned.1.call-done) | copy-start | bytes 6291460
  199.9 252.1 %all-gather.18.cloned.1.call-start = ((), (), s32[]{:S(2)}) async-start(), calls=%async_computation.18 | async-start | bytes 5947392 | tf_op jit(solution)/shard_map/all_gather | solution.py:181
  200.6 72.4 %copy-start.14 = (f32[2048]{0:T(1024)S(1)}, f32[2048]{0:T(1024)}, u32[]{:S(2)}) copy-start(f32[2048]{0:T(1024)} %param.26) | copy-start | bytes 24580
  200.6 365.2 %all-reduce.9.cloned.1.call-start = ((), (), s32[]{:S(2)}) async-start(), calls=%async_computation.20 | async-start | bytes 8388608 | tf_op jit(solution)/shard_map/psum | solution.py:205
  474.0 218.0 %reduce-scatter.9.cloned.1.call-start = ((), (), s32[]{:S(2)}) async-start(), calls=%async_computation.19 | async-start | bytes 2621440 | tf_op jit(solution)/shard_map/reduce_scatter | solution.py:187
  482.1 231.8 %all-reduce.11.cloned.1.call-start = ((), (), s32[]{:S(2)}) async-start(), calls=%async_computation.21 | async-start | bytes 4194304 | tf_op jit(solution)/shard_map/psum | solution.py:261
  655.2 139.7 %reduce-scatter.13.cloned.1.call-start = ((), (), s32[]{:S(2)}) async-start(), calls=%async_computation.23 | async-start | bytes 540672 | tf_op jit(solution)/shard_map/reduce_scatter | solution.py:269
  657.1 217.6 %reduce-scatter.15.cloned.1.call-start = ((), (), s32[]{:S(2)}) async-start(), calls=%async_computation.24 | async-start | bytes 540672 | tf_op jit(solution)/shard_map/reduce_scatter | solution.py:272
  659.2 297.1 %reduce-scatter.11.cloned.1.call-start = ((), (), s32[]{:S(2)}) async-start(), calls=%async_computation.22 | async-start | bytes 2162688 | tf_op jit(solution)/shard_map/reduce_scatter | solution.py:266
  662.1 375.9 %reduce-scatter.17.cloned.1.call-start = ((), (), s32[]{:S(2)}) async-start(), calls=%async_computation.25 | async-start | bytes 2162688 | tf_op jit(solution)/shard_map/reduce_scatter | solution.py:275
  667.4 459.0 %reduce-scatter.19.cloned.1.call-start = ((), (), s32[]{:S(2)}) async-start(), calls=%async_computation.26 | async-start | bytes 5947392 | tf_op jit(solution)/shard_map/reduce_scatter | solution.py:210
  675.5 539.8 %reduce-scatter.21.cloned.1.call-start = ((), (), s32[]{:S(2)}) async-start(), calls=%async_computation.27 | async-start | bytes 5947392 | tf_op jit(solution)/shard_map/reduce_scatter | solution.py:213
  683.6 620.1 %reduce-scatter.23.cloned.1.call-start = ((), (), s32[]{:S(2)}) async-start(), calls=%async_computation.28 | async-start | bytes 5947392 | tf_op jit(solution)/shard_map/reduce_scatter | solution.py:216
  696.3 24.8 %all-to-all-start.2 = ((bf16[32,16,512]{2,1,0:T(8,128)(2,1)}), bf16[32,16,512]{2,1,0:T(8,128)(2,1)S(1)}, u32[]{:S(2)}, u32[]{:S(2)}) async-start(bf16[32,16,512]{2,1,0:T(8,128)(2,1)} %bitcast.14), calls=%async_computation.3 | async-start | bytes 1048576 | tf_op jit(solution)/shard_map/all_to_all | solution.py:283
  718.4 160.3 %copy-start.20 = (bf16[2048]{0:T(1024)(128)(2,1)S(1)}, bf16[2048]{0:T(1024)(128)(2,1)}, u32[]{:S(2)}) copy-start(bf16[2048]{0:T(1024)(128)(2,1)} %get-tuple-element.247) | copy-start | bytes 12292
  721.0 222.7 %all-to-all-start.4 = ((bf16[32,16,512]{2,1,0:T(8,128)(2,1)}), bf16[32,16,512]{2,1,0:T(8,128)(2,1)S(1)}, u32[]{:S(2)}, u32[]{:S(2)}) async-start(bf16[32,16,512]{2,1,0:T(8,128)(2,1)} %bitcast.24), calls=%async_computation.5 | async-start | bytes 1048576 | tf_op jit(solution)/shard_map/all_to_all | solution.py:284
  876.1 429.3 %copy-start.1 = (bf16[512,512]{1,0:T(8,128)(2,1)S(1)}, bf16[512,512]{1,0:T(8,128)(2,1)}, u32[]{:S(2)}) copy-start(bf16[512,512]{1,0:T(8,128)(2,1)} %param.17) | copy-start | bytes 1572868
  (24 other events, 188.3 us)
Sparse Core Ops, SparseCore 0:
  50.7 28.4 all-gather.19
  81.5 44.0 all-gather.9
  127.9 43.2 all-gather.11
  176.2 91.9 all-reduce.6
  270.6 48.3 all-gather.13
  321.3 47.4 all-gather.15
  371.1 29.7 all-gather.21
  403.4 48.4 all-gather.17
  474.1 91.7 all-reduce.8
  568.1 29.5 reduce-scatter.8
  655.3 58.5 all-reduce.10
  717.8 77.0 reduce-scatter.12
  798.4 76.3 reduce-scatter.14
  878.2 78.1 reduce-scatter.10
  959.8 78.2 reduce-scatter.16
  1041.7 84.7 reduce-scatter.18
  1130.5 84.7 reduce-scatter.20
  1218.9 84.7 reduce-scatter.22
where the time goes:
time: 1320 us; the launch traced here: 1310 us
  waiting for transfers between devices  860 us (65%)
  matrix products  170 us (13%)
  blocking collectives  131 us (10%)
  other arithmetic  55.9 us (4%)
  local copies, waits for them, and re-layouts  51.2 us (4%)
  starting transfers between devices  28.6 us (2%)
  between operations  16 us (1%)
    dot_general x77, matrix products, matmul(): return jnp.dot(left, right, preferred_element_type=jnp.float32)  170 us
    reduce_scatter x1, waiting for transfers between devices, body(): lax.psum_scatter(up_weight_grad.astype(jnp.bfloat16), 'row', scatter_dime...  87.2 us
    reduce_scatter x1, waiting for transfers between devices, body(): lax.psum_scatter(gate_weight_grad.astype(jnp.bfloat16), 'row', scatter_di...  86.9 us
    reduce_scatter x1, waiting for transfers between devices, body(): lax.psum_scatter(down_weight_grad.astype(jnp.bfloat16), 'row', scatter_di...  86.7 us
    psum x1, waiting for transfers between devices, body(): normed_grad_two = lax.psum(normed_terms_two, 'col')  83.7 us
    reduce_scatter x1, waiting for transfers between devices, body(): lax.psum_scatter(output_weight_grad.astype(jnp.bfloat16), 'row', scatter_...  80.2 us
    reduce_scatter x1, waiting for transfers between devices, body(): lax.psum_scatter(value_weight_grad.astype(jnp.bfloat16), 'row', scatter_d...  78.5 us
    psum x1, waiting for transfers between devices, body(): attn_full = lax.psum(attn_terms, 'col')  67.2 us
  transfers between devices with their start and end apart: 22, of which 18 were waited for; matrix products, arithmetic and copies ran while one was open for 18% of the time, Pallas kernels for 0%

commit v1 on v0

--- a/solution.py
+++ b/solution.py
@@ -176,7 +176,9 @@
     normed_two = (resid * inv_two * ffn_gain).astype(jnp.bfloat16)
     resid_part = lax.dynamic_slice_in_dim(resid, col_start, quarter, 1)
     gate_w, up_w, down_w = (
-        lax.all_gather(w_gate, "row", axis=0, tiled=True),
+        jnp.concatenate(
+            lax.all_to_all(jnp.stack([w_gate] * lax.axis_size("row")), "row", 0, 0), axis=0
+        ),
         lax.all_gather(w_up, "row", axis=0, tiled=True),
         lax.all_gather(w_down, "row", axis=0, tiled=True),
     )

time: 1320 us -> 1310 us (level)
  waiting for transfers between devices: 860 us -> 837 us
  transfers between devices with their start and end apart: 22 -> 23, of which waited for: 18 -> 19; matrix products, arithmetic and copies ran while one was open for 18% -> 19% of each run, Pallas kernels for 0% -> 0%
where the time goes in v1:
time: 1310 us; the launch traced here: 1300 us
  waiting for transfers between devices  837 us (64%)
  matrix products  172 us (13%)
  blocking collectives  131 us (10%)
  local copies, waits for them, and re-layouts  56.6 us (4%)
  other arithmetic  55.9 us (4%)
  starting transfers between devices  33.5 us (3%)
  between operations  16 us (1%)
    dot_general x77, matrix products, matmul(): return jnp.dot(left, right, preferred_element_type=jnp.float32)  172 us
    reduce_scatter x1, waiting for transfers between devices, body(): lax.psum_scatter(up_weight_grad.astype(jnp.bfloat16), 'row', scatter_dime...  87.1 us
    reduce_scatter x1, waiting for transfers between devices, body(): lax.psum_scatter(gate_weight_grad.astype(jnp.bfloat16), 'row', scatter_di...  86.8 us
    reduce_scatter x1, waiting for transfers between devices, body(): lax.psum_scatter(down_weight_grad.astype(jnp.bfloat16), 'row', scatter_di...  86.6 us
    psum x1, waiting for transfers between devices, body(): normed_grad_two = lax.psum(normed_terms_two, 'col')  83.7 us
    reduce_scatter x1, waiting for transfers between devices, body(): lax.psum_scatter(output_weight_grad.astype(jnp.bfloat16), 'row', scatter_...  80.2 us
    reduce_scatter x1, waiting for transfers between devices, body(): lax.psum_scatter(value_weight_grad.astype(jnp.bfloat16), 'row', scatter_d...  78.5 us
    unnamed x1, blocking collectives  64.4 us
  transfers between devices with their start and end apart: 23, of which 19 were waited for; matrix products, arithmetic and copies ran while one was open for 19% of the time, Pallas kernels for 0%

profile of v1, /device:TPU:0, one launch (start us, length us, event | category | flops | bytes accessed | tf_op | source)
XLA Modules:
  0.0 1301.4 jit_solution(4121244902759686115)
XLA Ops:
  16.6 8.4 all-to-all-start.1
  53.0 22.4 %all_gather.35 = bf16[2048,64]{1,0:T(8,128)(2,1)S(1)} all-gather(bf16[64,64]{1,0:T(8,128)(2,1)S(1)} %copy-done.19), channel_id=1, replica_groups=mesh['row'=32,'col'=4] {'row'}, dimensions={0}, use_global_device_ids=true | all-gather | bytes 270336 | tf_op jit(solution)/shard_map/all_gather | solution.py:130
  75.5 26.7 %all_gather.36 = bf16[2048,64]{1,0:T(8,128)(2,1)} all-gather(bf16[64,64]{1,0:T(8,128)(2,1)S(1)} %copy-done.20), channel_id=1, replica_groups=mesh['row'=32,'col'=4] {'row'}, dimensions={0}, use_global_device_ids=true | all-gather | bytes 270336 | tf_op jit(solution)/shard_map/all_gather | solution.py:131
  111.3 14.4 %all-gather.10.cloned.1.call-done = bf16[2048,512]{1,0:T(8,128)(2,1)} async-done(((bf16[64,512]{1,0:T(8,128)(2,1)}), bf16[2048,512]{1,0:T(8,128)(2,1)}) %all-gather.10.cloned.1.call-update) | async-done | bytes 2097168 | tf_op jit(solution)/shard_map/all_gather | solution.py:129
  130.2 25.2 %while.32 = (s32[]{:T(128)}, bf16[8,512,64]{1,2,0:T(8,128)(2,1)S(1)}, f32[8,512]{1,0:T(8,128)}, bf16[8,512,64]{2,1,0:T(8,128)(2,1)}, bf16[1,512,64]{2,1,0:T(8,12...) while((s32[]{:T(128)}, bf16[8,512,64]{1,2,0:T(8,128)(2,1)S(1)}, ...), condition=%wide.region_8.9_spmd.clone.clone, body=%wide.region_5.8_spmd.clone.sunk.clone | while | flops 69991936 | bytes 3629153 | solution.py:157
  155.4 15.8 %all-gather.12.cloned.1.call-done = bf16[2048,512]{1,0:T(8,128)(2,1)} async-done(((bf16[64,512]{1,0:T(8,128)(2,1)}), bf16[2048,512]{1,0:T(8,128)(2,1)}) %all-gather.12.cloned.1.call-update) | async-done | bytes 2097168 | tf_op jit(solution)/shard_map/all_gather | solution.py:132
  179.8 17.0 %all_to_all.65 = bf16[32,16,512]{2,1,0:T(8,128)(2,1)S(1)} all-to-all(bf16[32,16,512]{2,1,0:T(8,128)(2,1)} %bitcast.196), channel_id=1, replica_groups=mesh['row'=32,'col'=4] {'row'}, dimensions={0} | all-to-all | bytes 1048576 | tf_op jit(solution)/shard_map/all_to_all | solution.py:120
  210.6 57.6 %all-reduce.7.cloned.1.call-done = f32[512,2048]{1,0:T(8,128)} async-done(((f32[512,2048]{1,0:T(8,128)}), f32[512,2048]{1,0:T(8,128)}) %all-reduce.7.cloned.1.call-update) | async-done | bytes 4194320 | tf_op jit(solution)/shard_map/psum | solution.py:173
  281.8 8.3 fusion.76
  290.1 28.8 %all-gather.14.cloned.1.call-done = bf16[2048,1408]{1,0:T(8,128)(2,1)} async-done(((bf16[64,1408]{1,0:T(8,128)(2,1)}), bf16[2048,1408]{1,0:T(8,128)(2,1)}) %all-gather.14.cloned.1.call-update) | async-done | bytes 5767184 | tf_op jit(solution)/shard_map/all_gather | solution.py:182
  318.9 8.2 fusion.77
  327.1 23.8 %all-gather.22.cloned.1.call-done = bf16[512,2048]{1,0:T(8,128)(2,1)} async-done(((bf16[512,512]{1,0:T(8,128)(2,1)}), bf16[512,2048]{1,0:T(8,128)(2,1)}) %all-gather.22.cloned.1.call-update) | async-done | bytes 2097168 | tf_op jit(solution)/shard_map/all_gather | solution.py:126
  350.9 51.0 %all-gather.16.cloned.1.call-done = bf16[2048,1408]{1,0:T(8,128)(2,1)} async-done(((bf16[64,1408]{1,0:T(8,128)(2,1)}), bf16[2048,1408]{1,0:T(8,128)(2,1)}) %all-gather.16.cloned.1.call-update) | async-done | bytes 5767184 | tf_op jit(solution)/shard_map/all_gather | solution.py:183
  401.9 11.3 multiply_convert_fusion.3
  413.2 38.7 %all-gather.18.cloned.1.call-done = bf16[2048,1408]{1,0:T(8,128)(2,1)} async-done(((bf16[64,1408]{1,0:T(8,128)(2,1)}), bf16[2048,1408]{1,0:T(8,128)(2,1)}) %all-gather.18.cloned.1.call-update) | async-done | bytes 5767184 | tf_op jit(solution)/shard_map/all_gather | solution.py:194
  463.4 7.8 convolution_convert_fusion.5
  471.3 83.7 %all-reduce.9.cloned.1.call-done = f32[512,2048]{1,0:T(8,128)} async-done(((f32[512,2048]{1,0:T(8,128)}), f32[512,2048]{1,0:T(8,128)}) %all-reduce.9.cloned.1.call-update) | async-done | bytes 4194320 | tf_op jit(solution)/shard_map/psum | solution.py:207
  568.4 65.4 %while.33 = (s32[]{:T(128)}, f32[8,512,64]{1,2,0:T(8,128)}, f32[8,512,64]{1,2,0:T(8,128)}, f32[8,512,64]{1,2,0:T(8,128)}, bf16[8,512,64]{2,1,0:T(8,128)(2,1)}, /...) while((s32[]{:T(128)}, f32[8,512,64]{1,2,0:T(8,128)}, ...), condition=%wide.region_17.18_spmd.clone.clone, body=%wide.region_15.17_spmd.clone.sunk.clone | while | flops 170982912 | bytes 8994941 | solution.py:234
  656.6 8.0 convolution_convert_fusion.2
  664.7 8.1 convolution_convert_fusion.1
  673.1 7.9 convolution_convert_fusion
  685.4 7.3 all-to-all-start.3
  692.7 10.3 all-reduce.11.cloned.1.call-done
  710.1 7.3 all-to-all-start.5
  722.4 61.5 %reduce-scatter.13.cloned.1.call-done = bf16[64,64]{1,0:T(8,128)(2,1)} async-done(((bf16[2048,64]{1,0:T(8,128)(2,1)}), bf16[64,64]{1,0:T(8,128)(2,1)}) %reduce-scatter.13.cloned.1.call-update) | async-done | bytes 8208 | tf_op jit(solution)/shard_map/reduce_scatter | solution.py:271
  785.3 78.5 %reduce-scatter.15.cloned.1.call-done = bf16[64,64]{1,0:T(8,128)(2,1)} async-done(((bf16[2048,64]{1,0:T(8,128)(2,1)}), bf16[64,64]{1,0:T(8,128)(2,1)}) %reduce-scatter.15.cloned.1.call-update) | async-done | bytes 8208 | tf_op jit(solution)/shard_map/reduce_scatter | solution.py:274
  867.7 64.4 %all-reduce.2 = (bf16[2048]{0:T(1024)(128)(2,1)S(1)}, bf16[2048]{0:T(1024)(128)(2,1)S(1)}) all-reduce(bf16[2048]{0:T(1024)(128)(2,1)S(1)} %get-tuple-element.249, bf16[2048]{0:T(1024)(128)(2,1)S(1)} %copy-done.17), channel_id=5, replica_groups=mesh['row'=32,'col'=4] {'row'}, use_global_device_ids=true, to_apply=%region_23.24.clone | all-reduce | flops 4096 | bytes 16384
  935.4 10.1 reduce-scatter.11.cloned.1.call-done
  946.9 80.2 %reduce-scatter.17.cloned.1.call-done = bf16[64,512]{1,0:T(8,128)(2,1)} async-done(((bf16[2048,512]{1,0:T(8,128)(2,1)}), bf16[64,512]{1,0:T(8,128)(2,1)}) %reduce-scatter.17.cloned.1.call-update) | async-done | bytes 65552 | tf_op jit(solution)/shard_map/reduce_scatter | solution.py:277
  1028.6 86.8 %reduce-scatter.19.cloned.1.call-done = bf16[64,1408]{1,0:T(8,128)(2,1)} async-done(((bf16[2048,1408]{1,0:T(8,128)(2,1)}), bf16[64,1408]{1,0:T(8,128)(2,1)}) %reduce-scatter.19.cloned.1.call-update) | async-done | bytes 180240 | tf_op jit(solution)/shard_map/reduce_scatter | solution.py:212
  1117.1 87.1 %reduce-scatter.21.cloned.1.call-done = bf16[64,1408]{1,0:T(8,128)(2,1)} async-done(((bf16[2048,1408]{1,0:T(8,128)(2,1)}), bf16[64,1408]{1,0:T(8,128)(2,1)}) %reduce-scatter.21.cloned.1.call-update) | async-done | bytes 180240 | tf_op jit(solution)/shard_map/reduce_scatter | solution.py:215
  1205.8 86.6 %reduce-scatter.23.cloned.1.call-done = bf16[64,1408]{1,0:T(8,128)(2,1)} async-done(((bf16[2048,1408]{1,0:T(8,128)(2,1)}), bf16[64,1408]{1,0:T(8,128)(2,1)}) %reduce-scatter.23.cloned.1.call-update) | async-done | bytes 180240 | tf_op jit(solution)/shard_map/reduce_scatter | solution.py:218
  (293 shorter events, 257.4 us)
Async XLA Ops:
  12.3 38.3 %copy-start.14 = (s32[1024]{0:T(1024)}, s32[1024]{0:T(1024)S(1)}, u32[]{:S(2)}) copy-start(s32[1024]{0:T(1024)S(1)} %pad_clamp_fusion.3) | copy-start | bytes 12292
  16.6 15.7 %all-to-all-start.1 = ((s32[32,16,1]{1,2,0:T(1,128)}), s32[32,16,1]{1,2,0:T(1,128)S(1)}, u32[]{:S(2)}, u32[]{:S(2)}) async-start(s32[32,16,1]{1,2,0:T(1,128)} %bitcast.2), calls=%async_computation.1 | async-start | bytes 32768 | tf_op jit(solution)/shard_map/all_to_all | solution.py:121
  27.7 47.8 %copy-start.20 = (bf16[64,64]{1,0:T(8,128)(2,1)S(1)}, bf16[64,64]{1,0:T(8,128)(2,1)}, u32[]{:S(2)}) copy-start(bf16[64,64]{1,0:T(8,128)(2,1)} %param.24) | copy-start | bytes 24580
  32.3 15.7 %all-to-all-start = ((bf16[32,16,512]{2,1,0:T(8,128)(2,1)}), bf16[32,16,512]{2,1,0:T(8,128)(2,1)S(1)}, u32[]{:S(2)}, u32[]{:S(2)}) async-start(bf16[32,16,512]{2,1,0:T(8,128)(2,1)} %bitcast), calls=%async_computation | async-start | bytes 1048576 | tf_op jit(solution)/shard_map/all_to_all | solution.py:119
  36.2 66.3 %all-gather.20.cloned.1.call-start = ((), (), s32[]{:S(2)}) async-start(), calls=%async_computation.30 | async-start | bytes 2621440 | tf_op jit(solution)/shard_map/all_gather | solution.py:125
  48.0 56.8 %copy-start.21 = (f32[2048]{0:T(1024)S(1)}, f32[2048]{0:T(1024)}, u32[]{:S(2)}) copy-start(f32[2048]{0:T(1024)} %param.21) | copy-start | bytes 24580
  50.6 75.0 %all-gather.10.cloned.1.call-start = ((), (), s32[]{:S(2)}) async-start(), calls=%async_computation.14 | async-start | bytes 2162688 | tf_op jit(solution)/shard_map/all_gather | solution.py:129
  51.4 119.8 %all-gather.12.cloned.1.call-start = ((), (), s32[]{:S(2)}) async-start(), calls=%async_computation.15 | async-start | bytes 2162688 | tf_op jit(solution)/shard_map/all_gather | solution.py:132
  52.1 216.1 %all-reduce.7.cloned.1.call-start = ((), (), s32[]{:S(2)}) async-start(), calls=%async_computation.16 | async-start | bytes 8388608 | tf_op jit(solution)/shard_map/psum | solution.py:173
  52.2 55.3 %copy-start.26 = (f32[32]{0:T(128)}, f32[32]{0:T(128)S(1)}, u32[]{:S(2)}) copy-start(f32[32]{0:T(128)S(1)} %negate_power_fusion) | copy-start | bytes 388
  53.0 54.6 %copy-start.13 = (f32[512]{0:T(512)}, f32[512]{0:T(512)S(1)}, u32[]{:S(2)}) copy-start(f32[512]{0:T(512)S(1)} %fusion.70) | copy-start | bytes 6148
  75.5 34.8 %copy-start.8 = (bf16[2048,64]{1,0:T(8,128)(2,1)}, bf16[2048,64]{1,0:T(8,128)(2,1)S(1)}, u32[]{:S(2)}) copy-start(bf16[2048,64]{1,0:T(8,128)(2,1)S(1)} %all_gather.35) | copy-start | bytes 786436
  176.1 142.8 %all-gather.14.cloned.1.call-start = ((), (), s32[]{:S(2)}) async-start(), calls=%async_computation.17 | async-start | bytes 5947392 | tf_op jit(solution)/shard_map/all_gather | solution.py:182
  176.7 174.3 %all-gather.22.cloned.1.call-start = ((), (), s32[]{:S(2)}) async-start(), calls=%async_computation.31 | async-start | bytes 2621440 | tf_op jit(solution)/shard_map/all_gather | solution.py:126
  199.6 202.3 %all-gather.16.cloned.1.call-start = ((), (), s32[]{:S(2)}) async-start(), calls=%async_computation.18 | async-start | bytes 5947392 | tf_op jit(solution)/shard_map/all_gather | solution.py:183
  200.4 251.5 %all-gather.18.cloned.1.call-start = ((), (), s32[]{:S(2)}) async-start(), calls=%async_computation.20 | async-start | bytes 5947392 | tf_op jit(solution)/shard_map/all_gather | solution.py:194
  205.3 76.5 %all-to-all-start.2 = ((bf16[32,64,1408]{2,1,0:T(8,128)(2,1)}), bf16[32,64,1408]{2,1,0:T(8,128)(2,1)}, u32[]{:S(2)}, u32[]{:S(2)}) async-start(bf16[32,64,1408]{2,1,0:T(8,128)(2,1)} %stack.2), calls=%async_computation.2 | async-start | bytes 11534336 | tf_op jit(solution)/shard_map/all_to_all | solution.py:180
  210.2 62.8 %copy-start.12 = (f32[2048]{0:T(1024)S(1)}, f32[2048]{0:T(1024)}, u32[]{:S(2)}) copy-start(f32[2048]{0:T(1024)} %param.26) | copy-start | bytes 24580
  210.2 344.8 %all-reduce.9.cloned.1.call-start = ((), (), s32[]{:S(2)}) async-start(), calls=%async_computation.21 | async-start | bytes 8388608 | tf_op jit(solution)/shard_map/psum | solution.py:207
  463.1 218.0 %reduce-scatter.9.cloned.1.call-start = ((), (), s32[]{:S(2)}) async-start(), calls=%async_computation.19 | async-start | bytes 2621440 | tf_op jit(solution)/shard_map/reduce_scatter | solution.py:189
  471.2 231.7 %all-reduce.11.cloned.1.call-start = ((), (), s32[]{:S(2)}) async-start(), calls=%async_computation.22 | async-start | bytes 4194304 | tf_op jit(solution)/shard_map/psum | solution.py:263
  644.3 139.7 %reduce-scatter.13.cloned.1.call-start = ((), (), s32[]{:S(2)}) async-start(), calls=%async_computation.24 | async-start | bytes 540672 | tf_op jit(solution)/shard_map/reduce_scatter | solution.py:271
  646.2 217.6 %reduce-scatter.15.cloned.1.call-start = ((), (), s32[]{:S(2)}) async-start(), calls=%async_computation.25 | async-start | bytes 540672 | tf_op jit(solution)/shard_map/reduce_scatter | solution.py:274
  648.3 297.1 %reduce-scatter.11.cloned.1.call-start = ((), (), s32[]{:S(2)}) async-start(), calls=%async_computation.23 | async-start | bytes 2162688 | tf_op jit(solution)/shard_map/reduce_scatter | solution.py:268
  651.2 375.9 %reduce-scatter.17.cloned.1.call-start = ((), (), s32[]{:S(2)}) async-start(), calls=%async_computation.26 | async-start | bytes 2162688 | tf_op jit(solution)/shard_map/reduce_scatter | solution.py:277
  656.6 458.8 %reduce-scatter.19.cloned.1.call-start = ((), (), s32[]{:S(2)}) async-start(), calls=%async_computation.27 | async-start | bytes 5947392 | tf_op jit(solution)/shard_map/reduce_scatter | solution.py:212
  664.6 539.5 %reduce-scatter.21.cloned.1.call-start = ((), (), s32[]{:S(2)}) async-start(), calls=%async_computation.28 | async-start | bytes 5947392 | tf_op jit(solution)/shard_map/reduce_scatter | solution.py:215
  672.8 619.7 %reduce-scatter.23.cloned.1.call-start = ((), (), s32[]{:S(2)}) async-start(), calls=%async_computation.29 | async-start | bytes 5947392 | tf_op jit(solution)/shard_map/reduce_scatter | solution.py:218
  685.4 24.7 %all-to-all-start.3 = ((bf16[32,16,512]{2,1,0:T(8,128)(2,1)}), bf16[32,16,512]{2,1,0:T(8,128)(2,1)S(1)}, u32[]{:S(2)}, u32[]{:S(2)}) async-start(bf16[32,16,512]{2,1,0:T(8,128)(2,1)} %bitcast.195), calls=%async_computation.4 | async-start | bytes 1048576 | tf_op jit(solution)/shard_map/all_to_all | solution.py:285
  707.4 160.3 %copy-start.17 = (bf16[2048]{0:T(1024)(128)(2,1)S(1)}, bf16[2048]{0:T(1024)(128)(2,1)}, u32[]{:S(2)}) copy-start(bf16[2048]{0:T(1024)(128)(2,1)} %get-tuple-element.247) | copy-start | bytes 12292
  710.1 222.7 %all-to-all-start.5 = ((bf16[32,16,512]{2,1,0:T(8,128)(2,1)}), bf16[32,16,512]{2,1,0:T(8,128)(2,1)S(1)}, u32[]{:S(2)}, u32[]{:S(2)}) async-start(bf16[32,16,512]{2,1,0:T(8,128)(2,1)} %bitcast.25), calls=%async_computation.6 | async-start | bytes 1048576 | tf_op jit(solution)/shard_map/all_to_all | solution.py:286
  865.1 429.0 %copy-start.1 = (bf16[512,512]{1,0:T(8,128)(2,1)S(1)}, bf16[512,512]{1,0:T(8,128)(2,1)}, u32[]{:S(2)}) copy-start(bf16[512,512]{1,0:T(8,128)(2,1)} %param.17) | copy-start | bytes 1572868
  (21 other events, 156.9 us)
Sparse Core Ops, SparseCore 0:
  50.7 28.4 all-gather.19
  81.5 44.0 all-gather.9
  127.9 43.2 all-gather.11
  176.2 91.9 all-reduce.6
  270.6 48.3 all-gather.13
  321.1 29.7 all-gather.21
  353.4 48.4 all-gather.15
  404.4 47.4 all-gather.17
  463.2 91.7 all-reduce.8
  557.2 29.5 reduce-scatter.8
  644.4 58.5 all-reduce.10
  706.8 77.0 reduce-scatter.12
  787.4 76.3 reduce-scatter.14
  867.2 78.2 reduce-scatter.10
  948.8 78.2 reduce-scatter.16
  1030.7 84.6 reduce-scatter.18
  1119.5 84.6 reduce-scatter.20
  1207.8 84.6 reduce-scatter.22
